TPU v7x, 128 devices: a whole 4x4x4 slice. The times are simulated.
128 devices in a mesh: orb: 128 (over y, x, z, core).
Axes of the slice: x: 4, y: 4, z: 4, core: 2. Of those that a mesh axis runs over, the one named last changes fastest.
Arguments:
- three_index: bfloat16 [128, 1024, 512], P('orb'), may hold values from -1 to 1
- ovl: bfloat16 [512, 512], replicated, may hold values from -1.5 to 1.6, as said below
- fock_virt: bfloat16 [512, 512], replicated, may hold values from -0.5 to 3.5, as said below
- fock_occ: float32 [128], replicated, may hold values from -1.2 to -0.4
- pair_partner: int32 [128, 4], P('orb'), may hold values from 0 to 127, as said below
- coup_pair: int32 [512, 2], P('orb'), may hold values from 0 to 511, as said below
- coup_fock: float32 [512, 2], P('orb'), may hold values from -1.2 to 1.2
- dom_blocks: int32 [512], P('orb'), may hold values from 1 to 2
Outputs:
- amplitudes: bfloat16 [512, 512, 512], P('orb')
- residual: float32 [512, 512, 512], P('orb')
- pair_energy: float32 [512], P('orb')
Inputs may be any that keep to these rules, and one draw needn't show every extreme that they name: `pair_partner`: row i names 4 different orbitals j, none equal to i, each with |j - i| <= 4; the first of them is exactly 4 away. `coup_pair`: pair g belongs to orbital g // 4. The 8 entries in the rows of one orbital's pairs name pairs of as many different other orbitals, each within 8 of it in orbital order; the first entry's orbital is exactly 8 away. `ovl`: diagonal between 0.8 and 1.2, small entries off it. `fock_virt`: diagonal between 0.3 and 3, small entries off it.
All inputs are finite; a program needn't handle non-finite values.
Results may differ from a plain program's by a relative error of at most 0.012.
The roundings to bfloat16 on the way count: a program that leaves them out, or rounds other values in their place, can miss the bound.
Values may be sent and summed in bfloat16 or wider, within the bound.
No kernel may reach another device: no remote copies, remote signals or barrier semaphores. Data moves between devices by JAX's collectives and lax.ppermute only.
A program may use at most 128 MiB of HBM per device.

v0:
```python
import jax
import jax.numpy as jnp
from jax import lax
from jax.sharding import PartitionSpec as P

ITERS = 2


def passed_along(block, axis, distance):
    devices = range(lax.axis_size(axis))
    route = [(i - distance, i) for i in devices if i - distance in devices]
    return lax.ppermute(block, axis, route)


def per_device(
    three_index, ovl, fock_virt, fock_occ, pair_partner, coup_pair, coup_fock, dom_blocks
):
    pair_count = pair_partner.shape[1]
    reach_span = max(8, pair_count * coup_pair.shape[1])
    virt_width = ovl.shape[0]
    own_index = lax.axis_index("orb")
    partner = pair_partner[0]
    partner_offset = partner - own_index
    block_offsets = list(range(-pair_count, 0)) + list(range(1, pair_count + 1))
    offset_list = list(range(-reach_span, 0)) + list(range(1, reach_span + 1))
    needed = jnp.zeros((pair_count, three_index.shape[1], virt_width), jnp.bfloat16)
    for offset in block_offsets:
        received = passed_along(three_index, "orb", -offset)
        needed = jnp.where((partner_offset == offset)[:, None, None], received, needed)
    pair_int = jnp.einsum("xa,pxb->pab", three_index[0], needed, preferred_element_type=jnp.float32)
    domain_size = dom_blocks * (virt_width // 2)
    inside = jnp.arange(virt_width)[None, :] < domain_size[:, None]
    domain_mask = (inside[:, :, None] & inside[:, None, :]).astype(jnp.float32)
    pair_int = domain_mask * pair_int
    virt_diag = jnp.diagonal(fock_virt).astype(jnp.float32)
    shift_occ = jnp.take(fock_occ, own_index) + jnp.take(fock_occ, partner)
    denominator = virt_diag[None, :, None] + virt_diag[None, None, :] - shift_occ[:, None, None]
    amplitudes = (-pair_int / denominator).astype(jnp.bfloat16)
    source_owner = coup_pair // pair_count
    local_slot = coup_pair % pair_count
    relative = source_owner - own_index
    fock_weights = []
    request_codes = []
    for offset in offset_list:
        fock_weights.append(jnp.sum(jnp.where(relative == offset, coup_fock, 0.0), axis=1))
        request_codes.append(jnp.sum(jnp.where(relative == offset, local_slot + 1, 0)))
    incoming = []
    for position, offset in enumerate(offset_list):
        arrived_code = passed_along(request_codes[position].reshape(1), "orb", offset)
        incoming.append(arrived_code[0])
    residual_out = jnp.zeros(pair_int.shape, jnp.float32)
    for sweep in range(ITERS):
        accumulated = jnp.zeros(pair_int.shape, jnp.float32)
        for position, offset in enumerate(offset_list):
            wanted = incoming[position]
            chosen = jnp.take(amplitudes, jnp.clip(wanted - 1, 0, pair_count - 1), axis=0)
            outgoing = jnp.where(wanted > 0, chosen, jnp.zeros_like(chosen))
            received = passed_along(outgoing, "orb", -offset)
            accumulated = (
                accumulated
                + fock_weights[position][:, None, None] * received.astype(jnp.float32)[None]
            )
        coupled = accumulated.astype(jnp.bfloat16)
        right_ovl = jnp.einsum(
            "pab,bc->pac", amplitudes, ovl, preferred_element_type=jnp.float32
        ).astype(jnp.bfloat16)
        left_ovl = jnp.einsum(
            "ab,pbc->pac", ovl, amplitudes, preferred_element_type=jnp.float32
        ).astype(jnp.bfloat16)
        coupled_ovl = jnp.einsum(
            "pab,bc->pac", coupled, ovl, preferred_element_type=jnp.float32
        ).astype(jnp.bfloat16)
        resid_pair = pair_int + jnp.einsum(
            "ab,pbc->pac", fock_virt, right_ovl, preferred_element_type=jnp.float32
        )
        resid_pair = resid_pair + jnp.einsum(
            "pab,bc->pac", left_ovl, fock_virt, preferred_element_type=jnp.float32
        )
        resid_pair = resid_pair - shift_occ[:, None, None] * jnp.einsum(
            "ab,pbc->pac", ovl, right_ovl, preferred_element_type=jnp.float32
        )
        resid_pair = resid_pair - jnp.einsum(
            "ab,pbc->pac", ovl, coupled_ovl, preferred_element_type=jnp.float32
        )
        residual_out = domain_mask * resid_pair
        amplitudes = (amplitudes.astype(jnp.float32) - residual_out / denominator).astype(
            jnp.bfloat16
        )
    energy = jnp.sum(pair_int * amplitudes.astype(jnp.float32), axis=(1, 2))
    return (amplitudes, residual_out, energy)


def solution(mesh):
    placed = (
        P("orb", None, None),
        P(),
        P(),
        P(),
        P("orb", None),
        P("orb", None),
        P("orb", None),
        P("orb"),
    )
    return jax.shard_map(
        per_device,
        mesh=mesh,
        in_specs=placed,
        out_specs=(P("orb", None, None), P("orb", None, None), P("orb")),
        check_vma=False,
    )
```

profile of v0, /device:TPU:71, one launch (start us, length us, event | category | flops | bytes accessed | tf_op | source)
XLA Modules:
  0.0 631.9 jit_solution(17626250402717887508)
XLA Ops:
  19.2 7.9 %gather_fusion = bf16[512]{0:T(512)(128)(2,1)S(1)} fusion(bf16[512,512]{1,0:T(8,128)(2,1)} %param.12, s32[512]{0:T(512)S(1)} %bitcast.231), kind=kCustom, calls=%fused_computation | custom fusion | bytes 6144 | tf_op jit(solution)/shard_map/jit(diagonal)/cond/branch_0_fun/gather | solution.py:35
  32.6 32.4 %collective-permute-start.16 = (s32[1]{0:T(128)}, s32[1]{0:T(128)}, u32[]{:S(2)}, u32[]{:S(2)}) collective-permute-start(s32[1]{0:T(128)} %bitcast.38), channel_id=1, source_target_pairs={{4,0},{5,1},{6,2},{7,3},{8,4},{9,5},{10,6},{11,7},{12,8},{13,9},{1... | collective-permute-start | bytes 20 | tf_op jit(solution)/shard_map/ppermute | solution.py:12
  69.5 6.0 collective-permute-done.14
  77.4 5.7 collective-permute-done.12
  86.9 6.3 collective-permute-start
  93.3 9.0 %collective-permute-start.7 = (bf16[1,1024,512]{2,1,0:T(8,128)(2,1)}, bf16[1,1024,512]{2,1,0:T(8,128)(2,1)}, u32[]{:S(2)}, u32[]{:S(2)}) collective-permute-start(bf16[1,1024,512]{2,1,0:T(8,128)(2,1)} %param.10), channel_id=1, source_target_pairs={{0,4},{1,5},{2,6},{3,7},{4,8},{5,9},{6,10},{7,11},{8,12},{9,13},{1... | collective-permute-start | bytes 3145736 | tf_op jit(solution)/shard_map/ppermute | solution.py:12
  118.0 9.4 %collective-permute-done.2 = bf16[1,1024,512]{2,1,0:T(8,128)(2,1)} collective-permute-done((bf16[1,1024,512]{2,1,0:T(8,128)(2,1)}, bf16[1,1024,512]{2,1,0:T(8,128)(2,1)}, u32[]{:S(2)}, u32[]{:S(2)}) %collective-permute-start.2) | collective-permute-done | bytes 1048608 | tf_op jit(solution)/shard_map/ppermute | solution.py:12
  129.6 29.5 %collective-permute-done.1 = bf16[1,1024,512]{2,1,0:T(8,128)(2,1)} collective-permute-done((bf16[1,1024,512]{2,1,0:T(8,128)(2,1)}, bf16[1,1024,512]{2,1,0:T(8,128)(2,1)}, u32[]{:S(2)}, u32[]{:S(2)}) %collective-permute-start.1) | collective-permute-done | bytes 1048608 | tf_op jit(solution)/shard_map/ppermute | solution.py:12
  161.5 18.2 %collective-permute-done = bf16[1,1024,512]{2,1,0:T(8,128)(2,1)} collective-permute-done((bf16[1,1024,512]{2,1,0:T(8,128)(2,1)}, bf16[1,1024,512]{2,1,0:T(8,128)(2,1)}, u32[]{:S(2)}, u32[]{:S(2)}) %collective-permute-start) | collective-permute-done | bytes 1048608 | tf_op jit(solution)/shard_map/ppermute | solution.py:12
  184.2 10.4 %fusion = (bf16[4,512,512]{1,2,0:T(8,128)(2,1)S(1)}, f32[4,512,512]{2,1,0:T(8,128)}) fusion(f32[4]{0:T(128)S(1)} %fusion.199, f32[512,512]{0,1:T(8,128)} %broadcast_add_fusion, pred[4,512]{1,0:T(4,128)(4,1)S(1)} %iota_compare_fusion, bf16[1,1024,512]{2,1,0:T(8,128)(2,1)} %param.10, pred[4]{0:T(512)(128)(4,1)S(1)} %get-tuple-element.107, ...), kind=kOutput, calls=%fused_computation.8 | convolution fusion | flops 2170552320 | bytes 16779312 | tf_op jit(solution)/shard_map/xa,pxb->pab/dot_general | solution.py:30
  197.9 9.4 %collective-permute-start.8 = (s32[1]{0:T(128)}, s32[1]{0:T(128)}, u32[]{:S(2)}, u32[]{:S(2)}) collective-permute-start(s32[1]{0:T(128)} %bitcast.22), channel_id=1, source_target_pairs={{8,0},{9,1},{10,2},{11,3},{12,4},{13,5},{14,6},{15,7},{16,8},{17,9... | collective-permute-start | bytes 20 | tf_op jit(solution)/shard_map/ppermute | solution.py:12
  211.1 8.3 %collective-permute-start.28 = (s32[1]{0:T(128)}, s32[1]{0:T(128)}, u32[]{:S(2)}, u32[]{:S(2)}) collective-permute-start(s32[1]{0:T(128)} %bitcast.62), channel_id=1, source_target_pairs={{0,3},{1,4},{2,5},{3,6},{4,7},{5,8},{6,9},{7,10},{8,11},{9,12},{10... | collective-permute-start | bytes 20 | tf_op jit(solution)/shard_map/ppermute | solution.py:12
  225.6 7.8 %collective-permute-start.24 = (s32[1]{0:T(128)}, s32[1]{0:T(128)}, u32[]{:S(2)}, u32[]{:S(2)}) collective-permute-start(s32[1]{0:T(128)} %bitcast.54), channel_id=1, source_target_pairs={{0,1},{1,2},{2,3},{3,4},{4,5},{5,6},{6,7},{7,8},{8,9},{9,10},{10,1... | collective-permute-start | bytes 20 | tf_op jit(solution)/shard_map/ppermute | solution.py:12
  242.6 11.1 %collective-permute-done.20 = s32[1]{0:T(128)} collective-permute-done((s32[1]{0:T(128)}, s32[1]{0:T(128)}, u32[]{:S(2)}, u32[]{:S(2)}) %collective-permute-start.20) | collective-permute-done | bytes 36 | tf_op jit(solution)/shard_map/ppermute | solution.py:12
  273.5 6.5 %collective-permute-start.30 = (s32[1]{0:T(128)}, s32[1]{0:T(128)}, u32[]{:S(2)}, u32[]{:S(2)}) collective-permute-start(s32[1]{0:T(128)} %bitcast.66), channel_id=1, source_target_pairs={{0,4},{1,5},{2,6},{3,7},{4,8},{5,9},{6,10},{7,11},{8,12},{9,13},{1... | collective-permute-start | bytes 20 | tf_op jit(solution)/shard_map/ppermute | solution.py:12
  284.1 8.0 %collective-permute-start.15 = (bf16[512,512]{0,1:T(8,128)(2,1)}, bf16[512,512]{0,1:T(8,128)(2,1)}, u32[]{:S(2)}, u32[]{:S(2)}) collective-permute-start(bf16[512,512]{0,1:T(8,128)(2,1)} %get-tuple-element.100), channel_id=1, source_target_pairs={{0,5},{1,6},{2,7},{3,8},{4,9},{5,10},{6,11},{7,12},{8,13},{9,14},{... | collective-permute-start | bytes 1572872 | tf_op jit(solution)/shard_map/ppermute | solution.py:12
  292.1 6.4 %collective-permute-start.11 = (bf16[512,512]{0,1:T(8,128)(2,1)}, bf16[512,512]{0,1:T(8,128)(2,1)}, u32[]{:S(2)}, u32[]{:S(2)}) collective-permute-start(bf16[512,512]{0,1:T(8,128)(2,1)} %get-tuple-element.91), channel_id=1, source_target_pairs={{0,7},{1,8},{2,9},{3,10},{4,11},{5,12},{6,13},{7,14},{8,15},{9,16}... | collective-permute-start | bytes 1572872 | tf_op jit(solution)/shard_map/ppermute | solution.py:12
  313.6 7.9 %collective-permute-done.15 = bf16[512,512]{0,1:T(8,128)(2,1)} collective-permute-done((bf16[512,512]{0,1:T(8,128)(2,1)}, bf16[512,512]{0,1:T(8,128)(2,1)}, u32[]{:S(2)}, u32[]{:S(2)}) %collective-permute-start.15) | collective-permute-done | bytes 524320 | tf_op jit(solution)/shard_map/ppermute | solution.py:12
  321.5 18.6 %collective-permute-start.23 = (bf16[512,512]{0,1:T(8,128)(2,1)S(1)}, bf16[512,512]{0,1:T(8,128)(2,1)}, u32[]{:S(2)}, u32[]{:S(2)}) collective-permute-start(bf16[512,512]{0,1:T(8,128)(2,1)S(1)} %copy-done.13), channel_id=1, source_target_pairs={{0,1},{1,2},{2,3},{3,4},{4,5},{5,6},{6,7},{7,8},{8,9},{9,10},{10,1... | collective-permute-start | bytes 1572872 | tf_op jit(solution)/shard_map/ppermute | solution.py:12
  340.1 5.6 collective-permute-start.21
  355.0 8.2 %collective-permute-start.39 = (bf16[512,512]{0,1:T(8,128)(2,1)}, bf16[512,512]{0,1:T(8,128)(2,1)}, u32[]{:S(2)}, u32[]{:S(2)}) collective-permute-start(bf16[512,512]{0,1:T(8,128)(2,1)} %get-tuple-element.86), channel_id=1, source_target_pairs={{8,0},{9,1},{10,2},{11,3},{12,4},{13,5},{14,6},{15,7},{16,8},{17,9... | collective-permute-start | bytes 1572872 | tf_op jit(solution)/shard_map/ppermute | solution.py:12
  421.0 19.7 %fusion.15 = bf16[4,512,512]{1,2,0:T(8,128)(2,1)} fusion(f32[4,512,512]{2,1,0:T(8,128)} %fusion.191, f32[4,512,512]{1,2,0:T(8,128)} %fusion.28, f32[4,512,512]{2,1,0:T(8,128)} %fusion.180, bf16[4,512,512]{1,2,0:T(8,128)(2,1)S(1)} %get-tuple-element.108, f32[4,512,512]{2,1,0:T(8,128)} %get-tuple-element.109, f32[4]{0:T(128)S(1)} %fusion.199, ...), kind=kOutput, calls=%fused_computation.32 | convolution fusion | flops 2195718144 | bytes 39323920 | tf_op jit(solution)/shard_map/ab,pbc->pac/dot_general | solution.py:82
  442.7 5.7 collective-permute-start.42
  451.6 4.9 collective-permute-start.44
  458.8 5.1 collective-permute-start.41
  469.1 27.2 %collective-permute-start.49 = (bf16[512,512]{0,1:T(8,128)(2,1)S(1)}, bf16[512,512]{0,1:T(8,128)(2,1)S(1)}, u32[]{:S(2)}, u32[]{:S(2)}) collective-permute-start(bf16[512,512]{0,1:T(8,128)(2,1)S(1)} %get-tuple-element.77), channel_id=1, source_target_pairs={{2,0},{3,1},{4,2},{5,3},{6,4},{7,5},{8,6},{9,7},{10,8},{11,9},{12,... | collective-permute-start | bytes 1572872 | tf_op jit(solution)/shard_map/ppermute | solution.py:12
  498.3 18.9 %collective-permute-start.47 = (bf16[512,512]{0,1:T(8,128)(2,1)S(1)}, bf16[512,512]{0,1:T(8,128)(2,1)}, u32[]{:S(2)}, u32[]{:S(2)}) collective-permute-start(bf16[512,512]{0,1:T(8,128)(2,1)S(1)} %get-tuple-element.79), channel_id=1, source_target_pairs={{0,1},{1,2},{2,3},{3,4},{4,5},{5,6},{6,7},{7,8},{8,9},{9,10},{10,1... | collective-permute-start | bytes 1572872 | tf_op jit(solution)/shard_map/ppermute | solution.py:12
  521.4 6.7 %collective-permute-start.40 = (bf16[512,512]{0,1:T(8,128)(2,1)S(1)}, bf16[512,512]{0,1:T(8,128)(2,1)}, u32[]{:S(2)}, u32[]{:S(2)}) collective-permute-start(bf16[512,512]{0,1:T(8,128)(2,1)S(1)} %get-tuple-element.69), channel_id=1, source_target_pairs={{0,8},{1,9},{2,10},{3,11},{4,12},{5,13},{6,14},{7,15},{8,16},{9,17... | collective-permute-start | bytes 1572872 | tf_op jit(solution)/shard_map/ppermute | solution.py:12
  539.2 6.8 %collective-permute-start.52 = (bf16[512,512]{0,1:T(8,128)(2,1)}, bf16[512,512]{0,1:T(8,128)(2,1)}, u32[]{:S(2)}, u32[]{:S(2)}) collective-permute-start(bf16[512,512]{0,1:T(8,128)(2,1)} %get-tuple-element.73), channel_id=1, source_target_pairs={{5,0},{6,1},{7,2},{8,3},{9,4},{10,5},{11,6},{12,7},{13,8},{14,9},{... | collective-permute-start | bytes 1572872 | tf_op jit(solution)/shard_map/ppermute | solution.py:12
  588.7 8.8 %collective-permute-done.51 = bf16[512,512]{0,1:T(8,128)(2,1)} collective-permute-done((bf16[512,512]{0,1:T(8,128)(2,1)}, bf16[512,512]{0,1:T(8,128)(2,1)}, u32[]{:S(2)}, u32[]{:S(2)}) %collective-permute-start.51) | collective-permute-done | bytes 524320 | tf_op jit(solution)/shard_map/ppermute | solution.py:12
  599.8 22.2 %multiply_reduce_fusion = (f32[4]{0:T(128)}, bf16[4,512,512]{1,2,0:T(8,128)(2,1)}, f32[4,512,512]{1,2,0:T(8,128)}) fusion(f32[4,512,512]{2,1,0:T(8,128)} %get-tuple-element.109, pred[4,512]{1,0:T(4,128)(4,1)S(1)} %iota_compare_fusion, f32[4]{0:T(128)S(1)} %fusion.199, f32[512,512]{0,1:T(8,128)} %broadcast_add_fusion, ...), kind=kOutput, calls=%fused_computation.20 | convolution fusion | flops 2198863872 | bytes 43518240 | tf_op jit(solution)/shard_map/ab,pbc->pac/dot_general | solution.py:82
  626.2 5.2 copy.112
  (186 shorter events, 245.2 us)
Async XLA Ops:
  0.6 84.3 %collective-permute-start.6 = (bf16[1,1024,512]{2,1,0:T(8,128)(2,1)}, bf16[1,1024,512]{2,1,0:T(8,128)(2,1)S(1)}, u32[]{:S(2)}, u32[]{:S(2)}) collective-permute-start(bf16[1,1024,512]{2,1,0:T(8,128)(2,1)} %param.10), channel_id=1, source_target_pairs={{0,3},{1,4},{2,5},{3,6},{4,7},{5,8},{6,9},{7,10},{8,11},{9,12},{10... | collective-permute-start | bytes 3145736 | tf_op jit(solution)/shard_map/ppermute | solution.py:12
  3.6 83.4 %collective-permute-start.5 = (bf16[1,1024,512]{2,1,0:T(8,128)(2,1)}, bf16[1,1024,512]{2,1,0:T(8,128)(2,1)}, u32[]{:S(2)}, u32[]{:S(2)}) collective-permute-start(bf16[1,1024,512]{2,1,0:T(8,128)(2,1)} %param.10), channel_id=1, source_target_pairs={{0,2},{1,3},{2,4},{3,5},{4,6},{5,7},{6,8},{7,9},{8,10},{9,11},{10,... | collective-permute-start | bytes 3145736 | tf_op jit(solution)/shard_map/ppermute | solution.py:12
  7.7 85.5 %collective-permute-start.4 = (bf16[1,1024,512]{2,1,0:T(8,128)(2,1)}, bf16[1,1024,512]{2,1,0:T(8,128)(2,1)}, u32[]{:S(2)}, u32[]{:S(2)}) collective-permute-start(bf16[1,1024,512]{2,1,0:T(8,128)(2,1)} %param.10), channel_id=1, source_target_pairs={{0,1},{1,2},{2,3},{3,4},{4,5},{5,6},{6,7},{7,8},{8,9},{9,10},{10,1... | collective-permute-start | bytes 3145736 | tf_op jit(solution)/shard_map/ppermute | solution.py:12
  9.9 105.8 %collective-permute-start.3 = (bf16[1,1024,512]{2,1,0:T(8,128)(2,1)}, bf16[1,1024,512]{2,1,0:T(8,128)(2,1)}, u32[]{:S(2)}, u32[]{:S(2)}) collective-permute-start(bf16[1,1024,512]{2,1,0:T(8,128)(2,1)} %param.10), channel_id=1, source_target_pairs={{1,0},{2,1},{3,2},{4,3},{5,4},{6,5},{7,6},{8,7},{9,8},{10,9},{11,1... | collective-permute-start | bytes 3145736 | tf_op jit(solution)/shard_map/ppermute | solution.py:12
  83.1 44.3 %collective-permute-start.2 = (bf16[1,1024,512]{2,1,0:T(8,128)(2,1)}, bf16[1,1024,512]{2,1,0:T(8,128)(2,1)}, u32[]{:S(2)}, u32[]{:S(2)}) collective-permute-start(bf16[1,1024,512]{2,1,0:T(8,128)(2,1)} %param.10), channel_id=1, source_target_pairs={{2,0},{3,1},{4,2},{5,3},{6,4},{7,5},{8,6},{9,7},{10,8},{11,9},{12,... | collective-permute-start | bytes 3145736 | tf_op jit(solution)/shard_map/ppermute | solution.py:12
  85.0 74.2 %collective-permute-start.1 = (bf16[1,1024,512]{2,1,0:T(8,128)(2,1)}, bf16[1,1024,512]{2,1,0:T(8,128)(2,1)}, u32[]{:S(2)}, u32[]{:S(2)}) collective-permute-start(bf16[1,1024,512]{2,1,0:T(8,128)(2,1)} %param.10), channel_id=1, source_target_pairs={{3,0},{4,1},{5,2},{6,3},{7,4},{8,5},{9,6},{10,7},{11,8},{12,9},{13... | collective-permute-start | bytes 3145736 | tf_op jit(solution)/shard_map/ppermute | solution.py:12
  86.9 92.7 %collective-permute-start = (bf16[1,1024,512]{2,1,0:T(8,128)(2,1)}, bf16[1,1024,512]{2,1,0:T(8,128)(2,1)}, u32[]{:S(2)}, u32[]{:S(2)}) collective-permute-start(bf16[1,1024,512]{2,1,0:T(8,128)(2,1)} %param.10), channel_id=1, source_target_pairs={{4,0},{5,1},{6,2},{7,3},{8,4},{9,5},{10,6},{11,7},{12,8},{13,9},{1... | collective-permute-start | bytes 3145736 | tf_op jit(solution)/shard_map/ppermute | solution.py:12
  93.3 88.7 %collective-permute-start.7 = (bf16[1,1024,512]{2,1,0:T(8,128)(2,1)}, bf16[1,1024,512]{2,1,0:T(8,128)(2,1)}, u32[]{:S(2)}, u32[]{:S(2)}) collective-permute-start(bf16[1,1024,512]{2,1,0:T(8,128)(2,1)} %param.10), channel_id=1, source_target_pairs={{0,4},{1,5},{2,6},{3,7},{4,8},{5,9},{6,10},{7,11},{8,12},{9,13},{1... | collective-permute-start | bytes 3145736 | tf_op jit(solution)/shard_map/ppermute | solution.py:12
  196.0 102.5 %collective-permute-start.13 = (bf16[512,512]{0,1:T(8,128)(2,1)}, bf16[512,512]{0,1:T(8,128)(2,1)S(1)}, u32[]{:S(2)}, u32[]{:S(2)}) collective-permute-start(bf16[512,512]{0,1:T(8,128)(2,1)} %get-tuple-element.97), channel_id=1, source_target_pairs={{0,6},{1,7},{2,8},{3,9},{4,10},{5,11},{6,12},{7,13},{8,14},{9,15},... | collective-permute-start | bytes 1572872 | tf_op jit(solution)/shard_map/ppermute | solution.py:12
  197.9 71.1 %collective-permute-start.8 = (s32[1]{0:T(128)}, s32[1]{0:T(128)}, u32[]{:S(2)}, u32[]{:S(2)}) collective-permute-start(s32[1]{0:T(128)} %bitcast.22), channel_id=1, source_target_pairs={{8,0},{9,1},{10,2},{11,3},{12,4},{13,5},{14,6},{15,7},{16,8},{17,9... | collective-permute-start | bytes 20 | tf_op jit(solution)/shard_map/ppermute | solution.py:12
  207.3 66.2 %collective-permute-start.38 = (s32[1]{0:T(128)}, s32[1]{0:T(128)}, u32[]{:S(2)}, u32[]{:S(2)}) collective-permute-start(s32[1]{0:T(128)} %bitcast.82), channel_id=1, source_target_pairs={{0,8},{1,9},{2,10},{3,11},{4,12},{5,13},{6,14},{7,15},{8,16},{9,17... | collective-permute-start | bytes 20 | tf_op jit(solution)/shard_map/ppermute | solution.py:12
  209.2 70.8 %collective-permute-start.36 = (s32[1]{0:T(128)}, s32[1]{0:T(128)}, u32[]{:S(2)}, u32[]{:S(2)}) collective-permute-start(s32[1]{0:T(128)} %bitcast.78), channel_id=1, source_target_pairs={{0,7},{1,8},{2,9},{3,10},{4,11},{5,12},{6,13},{7,14},{8,15},{9,16}... | collective-permute-start | bytes 20 | tf_op jit(solution)/shard_map/ppermute | solution.py:12
  292.1 48.0 %collective-permute-start.11 = (bf16[512,512]{0,1:T(8,128)(2,1)}, bf16[512,512]{0,1:T(8,128)(2,1)}, u32[]{:S(2)}, u32[]{:S(2)}) collective-permute-start(bf16[512,512]{0,1:T(8,128)(2,1)} %get-tuple-element.91), channel_id=1, source_target_pairs={{0,7},{1,8},{2,9},{3,10},{4,11},{5,12},{6,13},{7,14},{8,15},{9,16}... | collective-permute-start | bytes 1572872 | tf_op jit(solution)/shard_map/ppermute | solution.py:12
  298.5 47.2 %collective-permute-start.29 = (bf16[512,512]{0,1:T(8,128)(2,1)}, bf16[512,512]{0,1:T(8,128)(2,1)}, u32[]{:S(2)}, u32[]{:S(2)}) collective-permute-start(bf16[512,512]{0,1:T(8,128)(2,1)} %get-tuple-element.92), channel_id=1, source_target_pairs={{3,0},{4,1},{5,2},{6,3},{7,4},{8,5},{9,6},{10,7},{11,8},{12,9},{13... | collective-permute-start | bytes 1572872 | tf_op jit(solution)/shard_map/ppermute | solution.py:12
  309.7 45.3 %collective-permute-start.27 = (bf16[512,512]{0,1:T(8,128)(2,1)S(1)}, bf16[512,512]{0,1:T(8,128)(2,1)}, u32[]{:S(2)}, u32[]{:S(2)}) collective-permute-start(bf16[512,512]{0,1:T(8,128)(2,1)S(1)} %copy-done.15), channel_id=1, source_target_pairs={{2,0},{3,1},{4,2},{5,3},{6,4},{7,5},{8,6},{9,7},{10,8},{11,9},{12,... | collective-permute-start | bytes 1572872 | tf_op jit(solution)/shard_map/ppermute | solution.py:12
  311.6 51.5 %collective-permute-start.25 = (bf16[512,512]{0,1:T(8,128)(2,1)S(1)}, bf16[512,512]{0,1:T(8,128)(2,1)}, u32[]{:S(2)}, u32[]{:S(2)}) collective-permute-start(bf16[512,512]{0,1:T(8,128)(2,1)S(1)} %copy-done.14), channel_id=1, source_target_pairs={{1,0},{2,1},{3,2},{4,3},{5,4},{6,5},{7,6},{8,7},{9,8},{10,9},{11,1... | collective-permute-start | bytes 1572872 | tf_op jit(solution)/shard_map/ppermute | solution.py:12
  321.5 45.4 %collective-permute-start.23 = (bf16[512,512]{0,1:T(8,128)(2,1)S(1)}, bf16[512,512]{0,1:T(8,128)(2,1)}, u32[]{:S(2)}, u32[]{:S(2)}) collective-permute-start(bf16[512,512]{0,1:T(8,128)(2,1)S(1)} %copy-done.13), channel_id=1, source_target_pairs={{0,1},{1,2},{2,3},{3,4},{4,5},{5,6},{6,7},{7,8},{8,9},{9,10},{10,1... | collective-permute-start | bytes 1572872 | tf_op jit(solution)/shard_map/ppermute | solution.py:12
  355.0 54.6 %collective-permute-start.39 = (bf16[512,512]{0,1:T(8,128)(2,1)}, bf16[512,512]{0,1:T(8,128)(2,1)}, u32[]{:S(2)}, u32[]{:S(2)}) collective-permute-start(bf16[512,512]{0,1:T(8,128)(2,1)} %get-tuple-element.86), channel_id=1, source_target_pairs={{8,0},{9,1},{10,2},{11,3},{12,4},{13,5},{14,6},{15,7},{16,8},{17,9... | collective-permute-start | bytes 1572872 | tf_op jit(solution)/shard_map/ppermute | solution.py:12
  363.2 48.8 %collective-permute-start.37 = (bf16[512,512]{0,1:T(8,128)(2,1)}, bf16[512,512]{0,1:T(8,128)(2,1)}, u32[]{:S(2)}, u32[]{:S(2)}) collective-permute-start(bf16[512,512]{0,1:T(8,128)(2,1)} %get-tuple-element.87), channel_id=1, source_target_pairs={{7,0},{8,1},{9,2},{10,3},{11,4},{12,5},{13,6},{14,7},{15,8},{16,9}... | collective-permute-start | bytes 1572872 | tf_op jit(solution)/shard_map/ppermute | solution.py:12
  366.9 47.3 %collective-permute-start.35 = (bf16[512,512]{0,1:T(8,128)(2,1)}, bf16[512,512]{0,1:T(8,128)(2,1)}, u32[]{:S(2)}, u32[]{:S(2)}) collective-permute-start(bf16[512,512]{0,1:T(8,128)(2,1)} %get-tuple-element.88), channel_id=1, source_target_pairs={{6,0},{7,1},{8,2},{9,3},{10,4},{11,5},{12,6},{13,7},{14,8},{15,9},... | collective-permute-start | bytes 1572872 | tf_op jit(solution)/shard_map/ppermute | solution.py:12
  368.8 47.6 %collective-permute-start.33 = (bf16[512,512]{0,1:T(8,128)(2,1)}, bf16[512,512]{0,1:T(8,128)(2,1)}, u32[]{:S(2)}, u32[]{:S(2)}) collective-permute-start(bf16[512,512]{0,1:T(8,128)(2,1)} %get-tuple-element.89), channel_id=1, source_target_pairs={{5,0},{6,1},{7,2},{8,3},{9,4},{10,5},{11,6},{12,7},{13,8},{14,9},{... | collective-permute-start | bytes 1572872 | tf_op jit(solution)/shard_map/ppermute | solution.py:12
  373.4 45.2 %collective-permute-start.31 = (bf16[512,512]{0,1:T(8,128)(2,1)}, bf16[512,512]{0,1:T(8,128)(2,1)}, u32[]{:S(2)}, u32[]{:S(2)}) collective-permute-start(bf16[512,512]{0,1:T(8,128)(2,1)} %get-tuple-element.90), channel_id=1, source_target_pairs={{4,0},{5,1},{6,2},{7,3},{8,4},{9,5},{10,6},{11,7},{12,8},{13,9},{1... | collective-permute-start | bytes 1572872 | tf_op jit(solution)/shard_map/ppermute | solution.py:12
  451.6 44.7 %collective-permute-start.44 = (bf16[512,512]{0,1:T(8,128)(2,1)S(1)}, bf16[512,512]{0,1:T(8,128)(2,1)S(1)}, u32[]{:S(2)}, u32[]{:S(2)}) collective-permute-start(bf16[512,512]{0,1:T(8,128)(2,1)S(1)} %get-tuple-element.83), channel_id=1, source_target_pairs={{0,4},{1,5},{2,6},{3,7},{4,8},{5,9},{6,10},{7,11},{8,12},{9,13},{1... | collective-permute-start | bytes 1572872 | tf_op jit(solution)/shard_map/ppermute | solution.py:12
  456.4 41.8 %collective-permute-start.43 = (bf16[512,512]{0,1:T(8,128)(2,1)S(1)}, bf16[512,512]{0,1:T(8,128)(2,1)S(1)}, u32[]{:S(2)}, u32[]{:S(2)}) collective-permute-start(bf16[512,512]{0,1:T(8,128)(2,1)S(1)} %get-tuple-element.84), channel_id=1, source_target_pairs={{0,5},{1,6},{2,7},{3,8},{4,9},{5,10},{6,11},{7,12},{8,13},{9,14},{... | collective-permute-start | bytes 1572872 | tf_op jit(solution)/shard_map/ppermute | solution.py:12
  458.8 58.4 %collective-permute-start.41 = (bf16[512,512]{0,1:T(8,128)(2,1)S(1)}, bf16[512,512]{0,1:T(8,128)(2,1)S(1)}, u32[]{:S(2)}, u32[]{:S(2)}) collective-permute-start(bf16[512,512]{0,1:T(8,128)(2,1)S(1)} %get-tuple-element.75), channel_id=1, source_target_pairs={{0,7},{1,8},{2,9},{3,10},{4,11},{5,12},{6,13},{7,14},{8,15},{9,16}... | collective-permute-start | bytes 1572872 | tf_op jit(solution)/shard_map/ppermute | solution.py:12
  463.9 57.5 %collective-permute-start.50 = (bf16[512,512]{0,1:T(8,128)(2,1)S(1)}, bf16[512,512]{0,1:T(8,128)(2,1)S(1)}, u32[]{:S(2)}, u32[]{:S(2)}) collective-permute-start(bf16[512,512]{0,1:T(8,128)(2,1)S(1)} %get-tuple-element.76), channel_id=1, source_target_pairs={{3,0},{4,1},{5,2},{6,3},{7,4},{8,5},{9,6},{10,7},{11,8},{12,9},{13... | collective-permute-start | bytes 1572872 | tf_op jit(solution)/shard_map/ppermute | solution.py:12
  469.1 63.5 %collective-permute-start.49 = (bf16[512,512]{0,1:T(8,128)(2,1)S(1)}, bf16[512,512]{0,1:T(8,128)(2,1)S(1)}, u32[]{:S(2)}, u32[]{:S(2)}) collective-permute-start(bf16[512,512]{0,1:T(8,128)(2,1)S(1)} %get-tuple-element.77), channel_id=1, source_target_pairs={{2,0},{3,1},{4,2},{5,3},{6,4},{7,5},{8,6},{9,7},{10,8},{11,9},{12,... | collective-permute-start | bytes 1572872 | tf_op jit(solution)/shard_map/ppermute | solution.py:12
  533.4 46.3 %collective-permute-start.55 = (bf16[512,512]{0,1:T(8,128)(2,1)}, bf16[512,512]{0,1:T(8,128)(2,1)}, u32[]{:S(2)}, u32[]{:S(2)}) collective-permute-start(bf16[512,512]{0,1:T(8,128)(2,1)} %get-tuple-element.70), channel_id=1, source_target_pairs={{8,0},{9,1},{10,2},{11,3},{12,4},{13,5},{14,6},{15,7},{16,8},{17,9... | collective-permute-start | bytes 1572872 | tf_op jit(solution)/shard_map/ppermute | solution.py:12
  535.4 46.6 %collective-permute-start.54 = (bf16[512,512]{0,1:T(8,128)(2,1)}, bf16[512,512]{0,1:T(8,128)(2,1)}, u32[]{:S(2)}, u32[]{:S(2)}) collective-permute-start(bf16[512,512]{0,1:T(8,128)(2,1)} %get-tuple-element.71), channel_id=1, source_target_pairs={{7,0},{8,1},{9,2},{10,3},{11,4},{12,5},{13,6},{14,7},{15,8},{16,9}... | collective-permute-start | bytes 1572872 | tf_op jit(solution)/shard_map/ppermute | solution.py:12
  537.3 46.9 %collective-permute-start.53 = (bf16[512,512]{0,1:T(8,128)(2,1)}, bf16[512,512]{0,1:T(8,128)(2,1)}, u32[]{:S(2)}, u32[]{:S(2)}) collective-permute-start(bf16[512,512]{0,1:T(8,128)(2,1)} %get-tuple-element.72), channel_id=1, source_target_pairs={{6,0},{7,1},{8,2},{9,3},{10,4},{11,5},{12,6},{13,7},{14,8},{15,9},... | collective-permute-start | bytes 1572872 | tf_op jit(solution)/shard_map/ppermute | solution.py:12
  539.2 47.2 %collective-permute-start.52 = (bf16[512,512]{0,1:T(8,128)(2,1)}, bf16[512,512]{0,1:T(8,128)(2,1)}, u32[]{:S(2)}, u32[]{:S(2)}) collective-permute-start(bf16[512,512]{0,1:T(8,128)(2,1)} %get-tuple-element.73), channel_id=1, source_target_pairs={{5,0},{6,1},{7,2},{8,3},{9,4},{10,5},{11,6},{12,7},{13,8},{14,9},{... | collective-permute-start | bytes 1572872 | tf_op jit(solution)/shard_map/ppermute | solution.py:12
  546.1 51.5 %collective-permute-start.51 = (bf16[512,512]{0,1:T(8,128)(2,1)}, bf16[512,512]{0,1:T(8,128)(2,1)}, u32[]{:S(2)}, u32[]{:S(2)}) collective-permute-start(bf16[512,512]{0,1:T(8,128)(2,1)} %get-tuple-element.74), channel_id=1, source_target_pairs={{4,0},{5,1},{6,2},{7,3},{8,4},{9,5},{10,6},{11,7},{12,8},{13,9},{1... | collective-permute-start | bytes 1572872 | tf_op jit(solution)/shard_map/ppermute | solution.py:12
  (40 other events, 1237.6 us)
where the time goes:
time: 643 us; the launch traced here: 632 us
  starting transfers between devices  295 us (46%)
  waiting for transfers between devices  113 us (18%)
  local copies, waits for them, and re-layouts  109 us (17%)
  matrix products  76.6 us (12%)
  between operations  22.9 us (4%)
  other arithmetic  14.9 us (2%)
    ppermute x56, starting transfers between devices, passed_along(): return lax.ppermute(block, axis, route)  295 us
    ppermute x56, waiting for transfers between devices, passed_along(): return lax.ppermute(block, axis, route)  113 us
    convert_element_type x32, local copies, waits for them, and re-layouts, per_device(): received.astype(jnp.float32)[None]  71 us
    dot_general x2, matrix products, per_device(): jnp.einsum('ab,pbc->pac', ovl, coupled_ovl, preferred_element_type=jnp.fl...  41.9 us
    broadcast_in_dim x8, local copies, waits for them, and re-layouts, per_device(): jnp.where((partner_offset == offset)[:, None, None], received, needed)  17.4 us
  transfers between devices with their start and end apart: 56, of which 15 were waited for; matrix products, arithmetic and copies ran while one was open for 20% of the time, Pallas kernels for 0%

commit v1 on v0

v1 whole, which is shorter than its diff:
```python
import jax
import jax.numpy as jnp
from jax import lax
from jax.experimental import pallas as pl
from jax.experimental.pallas import tpu as pltpu
from jax.sharding import PartitionSpec as P


ITERS = 2
REACH = 8
HEAD = 16
OFFSETS = (4, -4, 8, -8, 3, -3, 7, -7, 5, -5, 6, -6, 2, -2, 1, -1)
EVEN = {-4: 0, -3: 7, -2: 1, -1: 2, 1: 3, 2: 5, 3: 4, 4: 6}
ODD = {-4: 0, -3: 2, -2: 1, -1: 3, 1: 4, 2: 5, 3: 8, 4: 6}


def shift(block, distance, cyclic=False):
    n = lax.axis_size("orb")
    route = [(i, (i + distance) % n) for i in range(n) if cyclic or 0 <= i + distance < n]
    return lax.ppermute(block, "orb", route)


def in_hbm(block):
    return pltpu.with_memory_space_constraint(block, pltpu.HBM)


def swap_cores(block):
    n = lax.axis_size("orb")
    return lax.ppermute(block, "orb", [(i, i ^ 1) for i in range(n)])


def domain_mask(size, shape):
    row = lax.broadcasted_iota(jnp.int32, shape, 0)
    col = lax.broadcasted_iota(jnp.int32, shape, 1)
    return (row < size) & (col < size)


def mm(a, b):
    return jnp.dot(a, b, preferred_element_type=jnp.float32)


def occupied_shift(own, partner_ref, occ_ref, pair):
    return occ_ref[own] + occ_ref[partner_ref[0, pair]]


def send_pair(own, code_ref, pair, buf, outs, sem):
    base = REACH + lax.rem(own, 2)
    for j, out in enumerate(outs):

        @pl.when(code_ref[base - OFFSETS[j]] == pair)
        def _():
            pltpu.make_async_copy(buf, out, sem.at[j]).start()


def finish_sends(own, code_ref, buf, outs, sem):
    base = REACH + lax.rem(own, 2)
    for j, out in enumerate(outs):

        @pl.when(code_ref[base - OFFSETS[j]] >= 0)
        def _():
            pltpu.make_async_copy(buf, out, sem.at[j]).wait()


def integral_kernel(own_ref, partner_ref, code_ref, dom_ref, occ_ref, at_ref, esum_ref, *rest):
    blocks = rest[:9]
    k_out, t_out = rest[9:11]
    outs = rest[11:-6]
    held, k_ref, t_ref, in_sem, out_sem, keep_sem = rest[-6:]
    own = own_ref[0]
    pairs, aux, width = held.shape

    def fetch(pair):
        offset = partner_ref[0, pair] - own
        even = lax.rem(own, 2) == 0
        for j, block in enumerate(blocks):
            match = jnp.zeros((), jnp.bool_)
            for d in EVEN:
                if EVEN[d] == j:
                    match = match | (even & (offset == d))
                if ODD[d] == j:
                    match = match | (~even & (offset == d))

            @pl.when(match)
            def _():
                pltpu.make_async_copy(
                    block.at[pl.ds(0, aux)], held.at[pair], in_sem.at[pair]
                ).start()

    def keep(pair):
        return (
            pltpu.make_async_copy(k_ref.at[pair], k_out.at[pair], keep_sem.at[2 * pair]),
            pltpu.make_async_copy(t_ref.at[pair], t_out.at[pair], keep_sem.at[2 * pair + 1]),
        )

    for pair in range(pairs):
        fetch(pair)
    for pair in range(pairs):
        pltpu.make_async_copy(
            blocks[0].at[pl.ds(0, aux)], held.at[pair], in_sem.at[pair]
        ).wait()
        integral = mm(at_ref[...], held[pair])
        mask = domain_mask(dom_ref[pair] * (width // 2), integral.shape)
        integral = jnp.where(mask, integral, 0.0)
        k_ref[pair] = integral
        denominator = esum_ref[...] - occupied_shift(own, partner_ref, occ_ref, pair)
        t_ref[pair] = (-integral / denominator).astype(jnp.bfloat16)
        send_pair(own, code_ref, pair, t_ref.at[pair], outs, out_sem)
        for copy in keep(pair):
            copy.start()
    finish_sends(own, code_ref, t_ref.at[0], outs, out_sem)
    for pair in range(pairs):
        for copy in keep(pair):
            copy.wait()


def partial_kernel(
    own_ref, partner_ref, occ_ref, dom_ref, k_ref, t_ref, ovl_ref, fock_ref, esum_ref,
    gain_ref, base_ref, part_ref=None
):
    own = own_ref[0]
    ovl = ovl_ref[...]
    fock = fock_ref[...]

    def step(pair, _):
        amp = t_ref[pair]
        right = mm(amp, ovl).astype(jnp.bfloat16)
        left = mm(ovl, amp).astype(jnp.bfloat16)
        resid = k_ref[pair] + mm(fock, right)
        resid = resid + mm(left, fock)
        shift_occ = occupied_shift(own, partner_ref, occ_ref, pair)
        resid = resid - shift_occ * mm(ovl, right)
        mask = domain_mask(dom_ref[pair] * (amp.shape[0] // 2), amp.shape)
        gain = jnp.where(mask, 1.0 / (esum_ref[...] - shift_occ), 0.0)
        gain_ref[pair] = gain
        base_ref[pair] = amp.astype(jnp.float32) - resid * gain
        if part_ref is not None:
            part_ref[pair] = jnp.where(mask, resid, 0.0)
        return 0

    lax.fori_loop(0, t_ref.shape[0], step, 0)


def update_kernel(
    own_ref, code_ref, place_ref, weight_ref, dom_ref, gain_ref, base_ref, ovl_ref, *rest, last
):
    rest = list(rest)
    if last:
        part_ref, k_ref = rest[:2]
        rest = rest[2:]
    blocks = rest[: len(OFFSETS)]
    rest = rest[len(OFFSETS) :]
    if last:
        tn_ref, resid_ref, energy_ref, held, in_sem, out_sem, tbuf, rbuf = rest
    else:
        tn_ref = rest[0]
        outs = rest[1:-3]
        held, in_sem, out_sem = rest[-3:]
    own = own_ref[0]
    pairs, width, _ = base_ref.shape

    middle = REACH + lax.rem(own, 2)
    for j, block in enumerate(blocks):
        entry = place_ref[middle + OFFSETS[j]]

        @pl.when(entry >= 0)
        def _():
            pltpu.make_async_copy(block, held.at[entry], in_sem.at[entry]).start()

    def results(pair):
        return (
            pltpu.make_async_copy(tbuf.at[pair], tn_ref.at[pair], out_sem.at[2 * pair]),
            pltpu.make_async_copy(rbuf.at[pair], resid_ref.at[pair], out_sem.at[2 * pair + 1]),
        )

    ovl = ovl_ref[...]
    for pair in range(pairs):
        for entry in (2 * pair, 2 * pair + 1):
            pltpu.make_async_copy(blocks[0], held.at[entry], in_sem.at[entry]).wait()
        first = held[2 * pair].astype(jnp.float32)
        second = held[2 * pair + 1].astype(jnp.float32)
        coupled = weight_ref[pair, 0] * first + weight_ref[pair, 1] * second
        cross = mm(coupled.astype(jnp.bfloat16), ovl).astype(jnp.bfloat16)
        term = mm(ovl, cross)
        amp = (base_ref[pair] + term * gain_ref[pair]).astype(jnp.bfloat16)
        if last:
            tbuf[pair] = amp
            mask = domain_mask(dom_ref[pair] * (width // 2), term.shape)
            rbuf[pair] = part_ref[pair] - jnp.where(mask, term, 0.0)
            for copy in results(pair):
                copy.start()
            energy_ref[pair] = jnp.sum(k_ref[pair] * amp.astype(jnp.float32))
        else:
            tn_ref[pair] = amp
            send_pair(own, code_ref, pair, tn_ref.at[pair], outs, out_sem)
    if last:
        for pair in range(pairs):
            for copy in results(pair):
                copy.wait()
    else:
        finish_sends(own, code_ref, tn_ref.at[0], outs, out_sem)


ANY = pl.BlockSpec(memory_space=pl.ANY)
SMEM = pl.BlockSpec(memory_space=pltpu.SMEM)
VMEM = pl.BlockSpec(memory_space=pltpu.VMEM)
HBM = pl.BlockSpec(memory_space=pltpu.HBM)


def params(mib):
    return pltpu.CompilerParams(vmem_limit_bytes=mib * 1024 * 1024)


def cost(flops, mib):
    return pl.CostEstimate(flops=flops, bytes_accessed=mib << 20, transcendentals=0)


def integrals(own, partner, code, dom, occ, at, esum, blocks):
    pairs = dom.shape[0]
    width, aux = at.shape
    nout = len(OFFSETS)
    one = jax.ShapeDtypeStruct((width, width), jnp.bfloat16)
    return pl.pallas_call(
        integral_kernel,
        in_specs=[SMEM] * 5 + [VMEM] * 2 + [ANY] * len(blocks),
        out_specs=[HBM] * 2 + [ANY] * nout,
        out_shape=[
            pltpu.HBM((pairs, width, width), jnp.float32),
            pltpu.HBM((pairs, width, width), jnp.bfloat16),
        ]
        + [one] * nout,
        scratch_shapes=[
            pltpu.VMEM((pairs, aux, width), jnp.bfloat16),
            pltpu.VMEM((pairs, width, width), jnp.float32),
            pltpu.VMEM((pairs, width, width), jnp.bfloat16),
            pltpu.SemaphoreType.DMA((pairs,)),
            pltpu.SemaphoreType.DMA((nout,)),
            pltpu.SemaphoreType.DMA((2 * pairs,)),
        ],
        compiler_params=params(16),
        cost_estimate=cost(2 * pairs * width * width * aux, 20),
        name="integrals",
    )(own, partner, code, dom, occ, at, esum, *blocks)


def partial_residual(own, partner, occ, dom, pair_int, amp, ovl, fock, esum, last):
    pairs, width, _ = amp.shape
    f32 = jax.ShapeDtypeStruct(pair_int.shape, jnp.float32)
    return pl.pallas_call(
        partial_kernel,
        in_specs=[SMEM] * 4 + [VMEM] * 5,
        out_specs=[VMEM] * (3 if last else 2),
        out_shape=[f32] * (3 if last else 2),
        compiler_params=params(20),
        cost_estimate=cost(10 * pairs * width**3, 20),
        name="partial",
    )(own, partner, occ, dom, pair_int, amp, ovl, fock, esum)


def update(own, code, place, weight, dom, terms, ovl, pair_int, blocks, last):
    pairs, width, _ = pair_int.shape
    f32 = jax.ShapeDtypeStruct((pairs, width, width), jnp.float32)
    b16 = jax.ShapeDtypeStruct((pairs, width, width), jnp.bfloat16)
    one = jax.ShapeDtypeStruct((width, width), jnp.bfloat16)
    nout = len(OFFSETS)

    def body(*refs):
        update_kernel(*refs, last=last)

    operands = [own, code, place, weight, dom, *terms[:2], ovl]
    scratch = [
        pltpu.VMEM((2 * pairs, width, width), jnp.bfloat16),
        pltpu.SemaphoreType.DMA((2 * pairs,)),
    ]
    if last:
        operands += [terms[2], pair_int]
        out_specs = [HBM] * 2 + [SMEM]
        out_shape = [b16, f32, jax.ShapeDtypeStruct((pairs,), jnp.float32)]
        scratch += [
            pltpu.SemaphoreType.DMA((2 * pairs,)),
            pltpu.VMEM(b16.shape, b16.dtype),
            pltpu.VMEM(f32.shape, f32.dtype),
        ]
    else:
        out_specs = [VMEM] + [ANY] * nout
        out_shape = [b16] + [one] * nout
        scratch += [pltpu.SemaphoreType.DMA((nout,))]
    return pl.pallas_call(
        body,
        in_specs=[SMEM] * 5 + [VMEM] * (len(operands) - 5) + [ANY] * len(blocks),
        out_specs=out_specs,
        out_shape=out_shape,
        scratch_shapes=scratch,
        compiler_params=params(20),
        cost_estimate=cost(4 * pairs * width**3, 20),
        name="update",
    )(*operands, *blocks)


def coupling_table(core, chips):
    rows = jnp.concatenate(
        [
            jnp.where(core == 0, jnp.stack([a, b]), jnp.stack([b, a])).reshape(2, -1)
            for a, b in chips
        ]
    )
    return jnp.concatenate([shift(rows, 6, True), rows, shift(rows, -6, True)])


def coupling_codes(own, core, table, listed_owner):
    table = table.astype(jnp.int32)
    half = table.shape[1] // 2
    owners, slots = table[:, :half], table[:, half:]
    code = jnp.sum(jnp.where(owners == own, slots + 1, 0), axis=1)
    orbital = own - core - REACH + jnp.arange(code.shape[0])
    code = jnp.where((orbital >= 0) & (orbital < lax.axis_size("orb")), code, 0) - 1
    position = jnp.where(listed_owner[None, :] == orbital[:, None], jnp.arange(1, half + 1), 0)
    return code, jnp.sum(position, axis=1) - 1


def per_device(
    three_index, ovl, fock_virt, fock_occ, pair_partner, coup_pair, coup_fock, dom_blocks
):
    n = lax.axis_size("orb")
    pairs = pair_partner.shape[1]
    aux, width = three_index.shape[1:]
    own = lax.axis_index("orb")
    core = lax.rem(own, 2)

    listed = coup_pair.reshape(-1)
    head = jnp.stack([listed // pairs, listed % pairs]).astype(jnp.bfloat16)
    entries = head.shape[1]
    block = jnp.concatenate(
        [three_index[0], jnp.pad(head, ((0, HEAD - 2), (0, width - entries)))]
    )
    below2 = shift(block, 2, True)
    above2 = shift(block, -2, True)
    mate = swap_cores(block)
    eye = jnp.arange(width)[:, None] == jnp.arange(width)[None, :]
    diag = jnp.where(eye, fock_virt.astype(jnp.float32), 0.0)
    esum = jnp.sum(diag, axis=1)[:, None] + jnp.sum(diag, axis=0)[None, :]
    at = three_index[0].T
    below4 = shift(below2, 2)
    above4 = shift(above2, -2)
    below2_mate = swap_cores(below2)
    above2_mate = swap_cores(above2)

    def header(x):
        return x[aux : aux + 2, :entries]

    table = coupling_table(
        core,
        [
            (header(below2), header(below2_mate)),
            (head, header(mate)),
            (header(above2), header(above2_mate)),
        ],
    )
    code, place = coupling_codes(own, core, table, listed // pairs)
    below3 = lax.ppermute(below4, "orb", [(i, i - 1) for i in range(1, n, 2)])
    above3 = lax.ppermute(above4, "orb", [(i, i + 1) for i in range(0, n, 2)])
    blocks = [below4, below2, below2_mate, mate, above2_mate, above2, above4, below3, above3]
    blocks = [in_hbm(b) for b in blocks]

    own1 = own.reshape(1)

    pair_int, amp, *outgoing = integrals(
        own1, pair_partner, code, dom_blocks, fock_occ, at, esum, blocks
    )
    for sweep in range(ITERS):
        last = sweep == ITERS - 1
        received = [shift(out, -d) for out, d in zip(outgoing, OFFSETS)]
        terms = partial_residual(
            own1, pair_partner, fock_occ, dom_blocks, pair_int, amp, ovl, fock_virt, esum, last
        )
        amp, *outgoing = update(
            own1, code, place, coup_fock, dom_blocks, terms, ovl, pair_int, received, last
        )
    residual, energy = outgoing
    return amp, residual, energy


def solution(mesh):
    placed = (
        P("orb", None, None),
        P(),
        P(),
        P(),
        P("orb", None),
        P("orb", None),
        P("orb", None),
        P("orb"),
    )

    return jax.shard_map(
        per_device,
        mesh=mesh,
        in_specs=placed,
        out_specs=(P("orb", None, None), P("orb", None, None), P("orb")),
        check_vma=False,
    )
```

time: 643 us -> 323 us (0.50)
  the two profiles are of different devices: /device:TPU:71 before, /device:TPU:28 now
where the time goes in v1:
time: 323 us; the launch traced here: 322 us
  starting transfers between devices  163 us (50%)
  waiting for transfers between devices  100 us (31%)
  Pallas kernels  35.8 us (11%)
  local copies, waits for them, and re-layouts  17.2 us (5%)
    ppermute x38, starting transfers between devices, shift(): return lax.ppermute(block, 'orb', route)  159 us
    ppermute x38, waiting for transfers between devices, shift(): return lax.ppermute(block, 'orb', route)  100 us
    pallas_call x2, Pallas kernels, partial_residual(): pl.pallas_call(partial_kernel, in_specs=[SMEM] * 4 + [VMEM] * 5, out_spec...  15.8 us
    pallas_call x2, Pallas kernels, update(): pl.pallas_call(body, in_specs=[SMEM] * 5 + [VMEM] * (len(operands) - 5) +...  13.1 us
    unnamed x48, local copies, waits for them, and re-layouts  12.3 us
    pallas_call x1, Pallas kernels, integrals(): pl.pallas_call(integral_kernel, in_specs=[SMEM] * 5 + [VMEM] * 2 + [ANY]...  6.94 us
  transfers between devices with their start and end apart: 43, of which 13 were waited for; matrix products, arithmetic and copies ran while one was open for 2% of the time, Pallas kernels for 5%

profile of v1, /device:TPU:28, one launch (start us, length us, event | category | flops | bytes accessed | tf_op | source)
XLA Modules:
  0.0 321.5 jit_solution(16479528984296652423)
XLA Ops:
  4.0 4.0 %collective-permute-start.3 = (bf16[1040,512]{1,0:T(8,128)(2,1)}, bf16[1040,512]{1,0:T(8,128)(2,1)}, u32[]{:S(2)}, u32[]{:S(2)}) collective-permute-start(bf16[1040,512]{1,0:T(8,128)(2,1)} %pad_maximum_fusion), channel_id=1, source_target_pairs={{0,126},{1,127},{2,0},{3,1},{4,2},{5,3},{6,4},{7,5},{8,6},{9,7},{1... | collective-permute-start | bytes 3194888 | tf_op jit(solution)/shard_map/ppermute | solution.py:20
  8.0 23.1 %collective-permute-done.3.rest_5_ = bf16[1040,512]{1,0:T(8,128)(2,1)} collective-permute-done((bf16[1040,512]{1,0:T(8,128)(2,1)}, bf16[1040,512]{1,0:T(8,128)(2,1)}, u32[]{:S(2)}, u32[]{:S(2)}) %collective-permute-start.3) | collective-permute-done | bytes 1064992 | tf_op jit(solution)/shard_map/ppermute | solution.py:20
  31.1 6.5 %collective-permute-start.8 = (bf16[1040,512]{1,0:T(8,128)(2,1)}, bf16[1040,512]{1,0:T(8,128)(2,1)}, u32[]{:S(2)}, u32[]{:S(2)}) collective-permute-start(bf16[1040,512]{1,0:T(8,128)(2,1)} %collective-permute-done.3.rest_5_), channel_id=1, source_target_pairs={{2,0},{3,1},{4,2},{5,3},{6,4},{7,5},{8,6},{9,7},{10,8},{11,9},{12,... | collective-permute-start | bytes 3194888 | tf_op jit(solution)/shard_map/ppermute | solution.py:20
  40.9 18.8 %collective-permute-done.8.rest_6_ = bf16[1040,512]{1,0:T(8,128)(2,1)} collective-permute-done((bf16[1040,512]{1,0:T(8,128)(2,1)}, bf16[1040,512]{1,0:T(8,128)(2,1)}, u32[]{:S(2)}, u32[]{:S(2)}) %collective-permute-start.8) | collective-permute-done | bytes 1064992 | tf_op jit(solution)/shard_map/ppermute | solution.py:20
  62.0 4.0 %collective-permute-done.7.rest_0_ = bf16[1040,512]{1,0:T(8,128)(2,1)} collective-permute-done((bf16[1040,512]{1,0:T(8,128)(2,1)}, bf16[1040,512]{1,0:T(8,128)(2,1)}, u32[]{:S(2)}, u32[]{:S(2)}) %collective-permute-start.7) | collective-permute-done | bytes 1064992 | tf_op jit(solution)/shard_map/ppermute | solution.py:20
  76.8 6.9 %integrals.1 = (f32[4,512,512]{2,1,0:T(8,128)}, bf16[4,512,512]{2,1,0:T(8,128)(2,1)}, bf16[512,512]{1,0:T(8,128)(2,1)S(1)}, bf16[512,512]{1,0:T(8,128)(2,1)S(1)}...) custom-call(s32[1]{0:T(128)} %bitcast.own_ref.refs_0_, ...), custom_call_target="tpu_custom_call" | custom-call | flops 2147483648 | bytes 20971520 | tf_op jit(solution)/shard_map/integrals/pallas_call | solution.py:222
  87.8 10.1 %collective-permute-start.11 = (bf16[512,512]{1,0:T(8,128)(2,1)S(1)}, bf16[512,512]{1,0:T(8,128)(2,1)S(1)}, u32[]{:S(2)}, u32[]{:S(2)}) collective-permute-start(bf16[512,512]{1,0:T(8,128)(2,1)S(1)} %get-tuple-element.47), channel_id=1, source_target_pairs={{4,0},{5,1},{6,2},{7,3},{8,4},{9,5},{10,6},{11,7},{12,8},{13,9},{1... | collective-permute-start | bytes 1572872 | tf_op jit(solution)/shard_map/ppermute | solution.py:20
  99.8 4.8 %collective-permute-start.13 = (bf16[512,512]{1,0:T(8,128)(2,1)S(1)}, bf16[512,512]{1,0:T(8,128)(2,1)S(1)}, u32[]{:S(2)}, u32[]{:S(2)}) collective-permute-start(bf16[512,512]{1,0:T(8,128)(2,1)S(1)} %get-tuple-element.49), channel_id=1, source_target_pairs={{8,0},{9,1},{10,2},{11,3},{12,4},{13,5},{14,6},{15,7},{16,8},{17,9... | collective-permute-start | bytes 1572872 | tf_op jit(solution)/shard_map/ppermute | solution.py:20
  106.6 5.8 %collective-permute-start.15 = (bf16[512,512]{1,0:T(8,128)(2,1)S(1)}, bf16[512,512]{1,0:T(8,128)(2,1)S(1)}, u32[]{:S(2)}, u32[]{:S(2)}) collective-permute-start(bf16[512,512]{1,0:T(8,128)(2,1)S(1)} %get-tuple-element.51), channel_id=1, source_target_pairs={{3,0},{4,1},{5,2},{6,3},{7,4},{8,5},{9,6},{10,7},{11,8},{12,9},{13... | collective-permute-start | bytes 1572872 | tf_op jit(solution)/shard_map/ppermute | solution.py:20
  112.4 4.7 %collective-permute-done.11.refs_8_ = bf16[512,512]{1,0:T(8,128)(2,1)S(1)} collective-permute-done((bf16[512,512]{1,0:T(8,128)(2,1)S(1)}, bf16[512,512]{1,0:T(8,128)(2,1)S(1)}, u32[]{:S(2)}, u32[]{:S(2)}) %collective-permute-start.11) | collective-permute-done | bytes 524320 | tf_op jit(solution)/shard_map/ppermute | solution.py:20
  119.6 6.4 %collective-permute-start.17 = (bf16[512,512]{1,0:T(8,128)(2,1)}, bf16[512,512]{1,0:T(8,128)(2,1)}, u32[]{:S(2)}, u32[]{:S(2)}) collective-permute-start(bf16[512,512]{1,0:T(8,128)(2,1)} %get-tuple-element.53), channel_id=1, source_target_pairs={{7,0},{8,1},{9,2},{10,3},{11,4},{12,5},{13,6},{14,7},{15,8},{16,9}... | collective-permute-start | bytes 1572872 | tf_op jit(solution)/shard_map/ppermute | solution.py:20
  126.0 9.7 %collective-permute-start.18 = (bf16[512,512]{1,0:T(8,128)(2,1)}, bf16[512,512]{1,0:T(8,128)(2,1)}, u32[]{:S(2)}, u32[]{:S(2)}) collective-permute-start(bf16[512,512]{1,0:T(8,128)(2,1)} %get-tuple-element.54), channel_id=1, source_target_pairs={{0,7},{1,8},{2,9},{3,10},{4,11},{5,12},{6,13},{7,14},{8,15},{9,16}... | collective-permute-start | bytes 1572872 | tf_op jit(solution)/shard_map/ppermute | solution.py:20
  139.2 5.1 %collective-permute-start.20 = (bf16[512,512]{1,0:T(8,128)(2,1)}, bf16[512,512]{1,0:T(8,128)(2,1)}, u32[]{:S(2)}, u32[]{:S(2)}) collective-permute-start(bf16[512,512]{1,0:T(8,128)(2,1)} %get-tuple-element.56), channel_id=1, source_target_pairs={{0,5},{1,6},{2,7},{3,8},{4,9},{5,10},{6,11},{7,12},{8,13},{9,14},{... | collective-permute-start | bytes 1572872 | tf_op jit(solution)/shard_map/ppermute | solution.py:20
  144.4 8.1 %collective-permute-done.16.refs_13_ = bf16[512,512]{1,0:T(8,128)(2,1)S(1)} collective-permute-done((bf16[512,512]{1,0:T(8,128)(2,1)S(1)}, bf16[512,512]{1,0:T(8,128)(2,1)S(1)}, u32[]{:S(2)}, u32[]{:S(2)}) %collective-permute-start.16) | collective-permute-done | bytes 524320 | tf_op jit(solution)/shard_map/ppermute | solution.py:20
  153.3 6.6 %collective-permute-start.21 = (bf16[512,512]{1,0:T(8,128)(2,1)}, bf16[512,512]{1,0:T(8,128)(2,1)}, u32[]{:S(2)}, u32[]{:S(2)}) collective-permute-start(bf16[512,512]{1,0:T(8,128)(2,1)} %get-tuple-element.57), channel_id=1, source_target_pairs={{6,0},{7,1},{8,2},{9,3},{10,4},{11,5},{12,6},{13,7},{14,8},{15,9},... | collective-permute-start | bytes 1572872 | tf_op jit(solution)/shard_map/ppermute | solution.py:20
  160.2 5.2 %collective-permute-start.22 = (bf16[512,512]{1,0:T(8,128)(2,1)}, bf16[512,512]{1,0:T(8,128)(2,1)}, u32[]{:S(2)}, u32[]{:S(2)}) collective-permute-start(bf16[512,512]{1,0:T(8,128)(2,1)} %copy-done.20), channel_id=1, source_target_pairs={{0,6},{1,7},{2,8},{3,9},{4,10},{5,11},{6,12},{7,13},{8,14},{9,15},... | collective-permute-start | bytes 1572872 | tf_op jit(solution)/shard_map/ppermute | solution.py:20
  171.3 4.1 %collective-permute-start.25 = (bf16[512,512]{1,0:T(8,128)(2,1)}, bf16[512,512]{1,0:T(8,128)(2,1)}, u32[]{:S(2)}, u32[]{:S(2)}) collective-permute-start(bf16[512,512]{1,0:T(8,128)(2,1)} %copy-done.17), channel_id=1, source_target_pairs={{1,0},{2,1},{3,2},{4,3},{5,4},{6,5},{7,6},{8,7},{9,8},{10,9},{11,1... | collective-permute-start | bytes 1572872 | tf_op jit(solution)/shard_map/ppermute | solution.py:20
  182.3 7.9 %partial.2 = (f32[4,512,512]{2,1,0:T(8,128)S(1)}, f32[4,512,512]{2,1,0:T(8,128)S(1)}) custom-call(s32[1]{0:T(128)} %bitcast.own_ref.refs_0_, s32[1,4]{1,0:T(1,128)S(1)} %copy-done.13, f32[128]{0:T(128)S(1)} %copy-done.14, s32[4]{0:T(128)S(1)} %copy-done.12, f32[4,512,512]{2,1,0:T(8,128)S(1)} %copy-done, bf16[4,512,512]{2,1,0:T(8,128)(2,1)S(1)} %copy-done.15, ...), custom_call_target="tpu_custom_call" | custom-call | flops 5368709120 | bytes 20971520 | tf_op jit(solution)/shard_map/partial/pallas_call | solution.py:248
  190.2 4.7 %collective-permute-done.22.refs_19_ = bf16[512,512]{1,0:T(8,128)(2,1)} collective-permute-done((bf16[512,512]{1,0:T(8,128)(2,1)}, bf16[512,512]{1,0:T(8,128)(2,1)}, u32[]{:S(2)}, u32[]{:S(2)}) %collective-permute-start.22) | collective-permute-done | bytes 524320 | tf_op jit(solution)/shard_map/ppermute | solution.py:20
  195.5 5.8 %update.2 = (bf16[4,512,512]{2,1,0:T(8,128)(2,1)S(1)}, bf16[512,512]{1,0:T(8,128)(2,1)S(1)}, bf16[512,512]{1,0:T(8,128)(2,1)S(1)}, bf16[512,512]{1,0:T(8,128)(2,...) custom-call(s32[1]{0:T(128)} %bitcast.own_ref.refs_0_, ...), custom_call_target="tpu_custom_call" | custom-call | flops 2147483648 | bytes 20971520 | tf_op jit(solution)/shard_map/update/pallas_call | solution.py:287
  201.4 6.2 %collective-permute-start.27 = (bf16[512,512]{1,0:T(8,128)(2,1)S(1)}, bf16[512,512]{1,0:T(8,128)(2,1)S(1)}, u32[]{:S(2)}, u32[]{:S(2)}) collective-permute-start(bf16[512,512]{1,0:T(8,128)(2,1)S(1)} %get-tuple-element.67), channel_id=1, source_target_pairs={{4,0},{5,1},{6,2},{7,3},{8,4},{9,5},{10,6},{11,7},{12,8},{13,9},{1... | collective-permute-start | bytes 1572872 | tf_op jit(solution)/shard_map/ppermute | solution.py:20
  209.5 6.9 %collective-permute-start.29 = (bf16[512,512]{1,0:T(8,128)(2,1)S(1)}, bf16[512,512]{1,0:T(8,128)(2,1)S(1)}, u32[]{:S(2)}, u32[]{:S(2)}) collective-permute-start(bf16[512,512]{1,0:T(8,128)(2,1)S(1)} %get-tuple-element.69), channel_id=1, source_target_pairs={{8,0},{9,1},{10,2},{11,3},{12,4},{13,5},{14,6},{15,7},{16,8},{17,9... | collective-permute-start | bytes 1572872 | tf_op jit(solution)/shard_map/ppermute | solution.py:20
  218.4 3.8 %collective-permute-start.31 = (bf16[512,512]{1,0:T(8,128)(2,1)S(1)}, bf16[512,512]{1,0:T(8,128)(2,1)S(1)}, u32[]{:S(2)}, u32[]{:S(2)}) collective-permute-start(bf16[512,512]{1,0:T(8,128)(2,1)S(1)} %get-tuple-element.71), channel_id=1, source_target_pairs={{3,0},{4,1},{5,2},{6,3},{7,4},{8,5},{9,6},{10,7},{11,8},{12,9},{13... | collective-permute-start | bytes 1572872 | tf_op jit(solution)/shard_map/ppermute | solution.py:20
  222.2 7.4 %collective-permute-done.27.refs_10_ = bf16[512,512]{1,0:T(8,128)(2,1)S(1)} collective-permute-done((bf16[512,512]{1,0:T(8,128)(2,1)S(1)}, bf16[512,512]{1,0:T(8,128)(2,1)S(1)}, u32[]{:S(2)}, u32[]{:S(2)}) %collective-permute-start.27) | collective-permute-done | bytes 524320 | tf_op jit(solution)/shard_map/ppermute | solution.py:20
  231.7 6.2 %collective-permute-start.33 = (bf16[512,512]{1,0:T(8,128)(2,1)S(1)}, bf16[512,512]{1,0:T(8,128)(2,1)S(1)}, u32[]{:S(2)}, u32[]{:S(2)}) collective-permute-start(bf16[512,512]{1,0:T(8,128)(2,1)S(1)} %get-tuple-element.73), channel_id=1, source_target_pairs={{7,0},{8,1},{9,2},{10,3},{11,4},{12,5},{13,6},{14,7},{15,8},{16,9}... | collective-permute-start | bytes 1572872 | tf_op jit(solution)/shard_map/ppermute | solution.py:20
  237.9 12.2 %collective-permute-start.34 = (bf16[512,512]{1,0:T(8,128)(2,1)S(1)}, bf16[512,512]{1,0:T(8,128)(2,1)S(1)}, u32[]{:S(2)}, u32[]{:S(2)}) collective-permute-start(bf16[512,512]{1,0:T(8,128)(2,1)S(1)} %get-tuple-element.74), channel_id=1, source_target_pairs={{0,7},{1,8},{2,9},{3,10},{4,11},{5,12},{6,13},{7,14},{8,15},{9,16}... | collective-permute-start | bytes 1572872 | tf_op jit(solution)/shard_map/ppermute | solution.py:20
  257.2 9.2 %collective-permute-done.32.refs_15_ = bf16[512,512]{1,0:T(8,128)(2,1)S(1)} collective-permute-done((bf16[512,512]{1,0:T(8,128)(2,1)S(1)}, bf16[512,512]{1,0:T(8,128)(2,1)S(1)}, u32[]{:S(2)}, u32[]{:S(2)}) %collective-permute-start.32) | collective-permute-done | bytes 524320 | tf_op jit(solution)/shard_map/ppermute | solution.py:20
  268.3 13.0 %collective-permute-start.38 = (bf16[512,512]{1,0:T(8,128)(2,1)S(1)}, bf16[512,512]{1,0:T(8,128)(2,1)S(1)}, u32[]{:S(2)}, u32[]{:S(2)}) collective-permute-start(bf16[512,512]{1,0:T(8,128)(2,1)S(1)} %get-tuple-element.78), channel_id=1, source_target_pairs={{0,6},{1,7},{2,8},{3,9},{4,10},{5,11},{6,12},{7,13},{8,14},{9,15},... | collective-permute-start | bytes 1572872 | tf_op jit(solution)/shard_map/ppermute | solution.py:20
  283.2 3.9 %collective-permute-start.40 = (bf16[512,512]{1,0:T(8,128)(2,1)S(1)}, bf16[512,512]{1,0:T(8,128)(2,1)S(1)}, u32[]{:S(2)}, u32[]{:S(2)}) collective-permute-start(bf16[512,512]{1,0:T(8,128)(2,1)S(1)} %get-tuple-element.80), channel_id=1, source_target_pairs={{0,2},{1,3},{2,4},{3,5},{4,6},{5,7},{6,8},{7,9},{8,10},{9,11},{10,... | collective-permute-start | bytes 1572872 | tf_op jit(solution)/shard_map/ppermute | solution.py:20
  289.1 12.5 %collective-permute-done.37.refs_20_ = bf16[512,512]{1,0:T(8,128)(2,1)S(1)} collective-permute-done((bf16[512,512]{1,0:T(8,128)(2,1)S(1)}, bf16[512,512]{1,0:T(8,128)(2,1)S(1)}, u32[]{:S(2)}, u32[]{:S(2)}) %collective-permute-start.37) | collective-permute-done | bytes 524320 | tf_op jit(solution)/shard_map/ppermute | solution.py:20
  303.5 7.9 %partial.3 = (f32[4,512,512]{2,1,0:T(8,128)S(1)}, f32[4,512,512]{2,1,0:T(8,128)S(1)}, f32[4,512,512]{2,1,0:T(8,128)S(1)}) custom-call(s32[1]{0:T(128)} %bitcast.own_ref.refs_0_, s32[1,4]{1,0:T(1,128)S(1)} %copy-done.13, f32[128]{0:T(128)S(1)} %copy-done.14, s32[4]{0:T(128)S(1)} %copy-done.12, f32[4,512,512]{2,1,0:T(8,128)S(1)} %copy-done.1, ...), custom_call_target="tpu_custom_call" | custom-call | flops 5368709120 | bytes 20971520 | tf_op jit(solution)/shard_map/partial/pallas_call | solution.py:248
  314.1 7.2 %update.3 = (bf16[4,512,512]{2,1,0:T(8,128)(2,1)}, f32[4,512,512]{2,1,0:T(8,128)}, f32[4]{0:T(128)}) custom-call(s32[1]{0:T(128)} %bitcast.own_ref.refs_0_, s32[18]{0:T(128)S(1)} %fusion.12.code_ref.refs_1_, s32[18]{0:T(128)S(1)} %broadcast_add_fusion.1.refs_2_, f32[4,2]{1,0:T(4,128)S(1)} %copy.22.refs_3_, s32[4]{0:T(128)S(1)} %copy-done.12, ...), custom_call_target="tpu_custom_call" | custom-call | flops 2147483648 | bytes 20971520 | tf_op jit(solution)/shard_map/update/pallas_call | solution.py:287
  (140 shorter events, 71.4 us)
Async XLA Ops:
  4.0 27.1 %collective-permute-start.3 = (bf16[1040,512]{1,0:T(8,128)(2,1)}, bf16[1040,512]{1,0:T(8,128)(2,1)}, u32[]{:S(2)}, u32[]{:S(2)}) collective-permute-start(bf16[1040,512]{1,0:T(8,128)(2,1)} %pad_maximum_fusion), channel_id=1, source_target_pairs={{0,126},{1,127},{2,0},{3,1},{4,2},{5,3},{6,4},{7,5},{8,6},{9,7},{1... | collective-permute-start | bytes 3194888 | tf_op jit(solution)/shard_map/ppermute | solution.py:20
  8.0 29.6 %collective-permute-start = (bf16[1040,512]{1,0:T(8,128)(2,1)}, bf16[1040,512]{1,0:T(8,128)(2,1)}, u32[]{:S(2)}, u32[]{:S(2)}) collective-permute-start(bf16[1040,512]{1,0:T(8,128)(2,1)} %pad_maximum_fusion), channel_id=1, source_target_pairs={{0,2},{1,3},{2,4},{3,5},{4,6},{5,7},{6,8},{7,9},{8,10},{9,11},{10,... | collective-permute-start | bytes 3194888 | tf_op jit(solution)/shard_map/ppermute | solution.py:20
  31.1 28.7 %collective-permute-start.8 = (bf16[1040,512]{1,0:T(8,128)(2,1)}, bf16[1040,512]{1,0:T(8,128)(2,1)}, u32[]{:S(2)}, u32[]{:S(2)}) collective-permute-start(bf16[1040,512]{1,0:T(8,128)(2,1)} %collective-permute-done.3.rest_5_), channel_id=1, source_target_pairs={{2,0},{3,1},{4,2},{5,3},{6,4},{7,5},{8,6},{9,7},{10,8},{11,9},{12,... | collective-permute-start | bytes 3194888 | tf_op jit(solution)/shard_map/ppermute | solution.py:20
  37.6 28.4 %collective-permute-start.7 = (bf16[1040,512]{1,0:T(8,128)(2,1)}, bf16[1040,512]{1,0:T(8,128)(2,1)}, u32[]{:S(2)}, u32[]{:S(2)}) collective-permute-start(bf16[1040,512]{1,0:T(8,128)(2,1)} %collective-permute-done.rest_1_), channel_id=1, source_target_pairs={{0,2},{1,3},{2,4},{3,5},{4,6},{5,7},{6,8},{7,9},{8,10},{9,11},{10,... | collective-permute-start | bytes 3194888 | tf_op jit(solution)/shard_map/ppermute | solution.py:20
  39.5 28.9 %collective-permute-start.2 = (bf16[1040,512]{1,0:T(8,128)(2,1)}, bf16[1040,512]{1,0:T(8,128)(2,1)}, u32[]{:S(2)}, u32[]{:S(2)}) collective-permute-start(bf16[1040,512]{1,0:T(8,128)(2,1)} %pad_maximum_fusion), channel_id=1, source_target_pairs={{0,1},{1,0},{2,3},{3,2},{4,5},{5,4},{6,7},{7,6},{8,9},{9,8},{10,11... | collective-permute-start | bytes 3194888 | tf_op jit(solution)/shard_map/ppermute | solution.py:29
  39.6 30.3 %collective-permute-start.4 = (bf16[1040,512]{1,0:T(8,128)(2,1)}, bf16[1040,512]{1,0:T(8,128)(2,1)}, u32[]{:S(2)}, u32[]{:S(2)}) collective-permute-start(bf16[1040,512]{1,0:T(8,128)(2,1)} %collective-permute-done.3.rest_5_), channel_id=1, source_target_pairs={{0,1},{1,0},{2,3},{3,2},{4,5},{5,4},{6,7},{7,6},{8,9},{9,8},{10,11... | collective-permute-start | bytes 3194888 | tf_op jit(solution)/shard_map/ppermute | solution.py:29
  40.1 30.6 %collective-permute-start.1 = (bf16[1040,512]{1,0:T(8,128)(2,1)}, bf16[1040,512]{1,0:T(8,128)(2,1)}, u32[]{:S(2)}, u32[]{:S(2)}) collective-permute-start(bf16[1040,512]{1,0:T(8,128)(2,1)} %collective-permute-done.rest_1_), channel_id=1, source_target_pairs={{0,1},{1,0},{2,3},{3,2},{4,5},{5,4},{6,7},{7,6},{8,9},{9,8},{10,11... | collective-permute-start | bytes 3194888 | tf_op jit(solution)/shard_map/ppermute | solution.py:29
  87.8 29.3 %collective-permute-start.11 = (bf16[512,512]{1,0:T(8,128)(2,1)S(1)}, bf16[512,512]{1,0:T(8,128)(2,1)S(1)}, u32[]{:S(2)}, u32[]{:S(2)}) collective-permute-start(bf16[512,512]{1,0:T(8,128)(2,1)S(1)} %get-tuple-element.47), channel_id=1, source_target_pairs={{4,0},{5,1},{6,2},{7,3},{8,4},{9,5},{10,6},{11,7},{12,8},{13,9},{1... | collective-permute-start | bytes 1572872 | tf_op jit(solution)/shard_map/ppermute | solution.py:20
  99.8 26.1 %collective-permute-start.13 = (bf16[512,512]{1,0:T(8,128)(2,1)S(1)}, bf16[512,512]{1,0:T(8,128)(2,1)S(1)}, u32[]{:S(2)}, u32[]{:S(2)}) collective-permute-start(bf16[512,512]{1,0:T(8,128)(2,1)S(1)} %get-tuple-element.49), channel_id=1, source_target_pairs={{8,0},{9,1},{10,2},{11,3},{12,4},{13,5},{14,6},{15,7},{16,8},{17,9... | collective-permute-start | bytes 1572872 | tf_op jit(solution)/shard_map/ppermute | solution.py:20
  104.7 31.0 %collective-permute-start.14 = (bf16[512,512]{1,0:T(8,128)(2,1)S(1)}, bf16[512,512]{1,0:T(8,128)(2,1)S(1)}, u32[]{:S(2)}, u32[]{:S(2)}) collective-permute-start(bf16[512,512]{1,0:T(8,128)(2,1)S(1)} %get-tuple-element.50), channel_id=1, source_target_pairs={{0,8},{1,9},{2,10},{3,11},{4,12},{5,13},{6,14},{7,15},{8,16},{9,17... | collective-permute-start | bytes 1572872 | tf_op jit(solution)/shard_map/ppermute | solution.py:20
  106.6 31.9 %collective-permute-start.15 = (bf16[512,512]{1,0:T(8,128)(2,1)S(1)}, bf16[512,512]{1,0:T(8,128)(2,1)S(1)}, u32[]{:S(2)}, u32[]{:S(2)}) collective-permute-start(bf16[512,512]{1,0:T(8,128)(2,1)S(1)} %get-tuple-element.51), channel_id=1, source_target_pairs={{3,0},{4,1},{5,2},{6,3},{7,4},{8,5},{9,6},{10,7},{11,8},{12,9},{13... | collective-permute-start | bytes 1572872 | tf_op jit(solution)/shard_map/ppermute | solution.py:20
  117.1 35.4 %collective-permute-start.16 = (bf16[512,512]{1,0:T(8,128)(2,1)S(1)}, bf16[512,512]{1,0:T(8,128)(2,1)S(1)}, u32[]{:S(2)}, u32[]{:S(2)}) collective-permute-start(bf16[512,512]{1,0:T(8,128)(2,1)S(1)} %get-tuple-element.52), channel_id=1, source_target_pairs={{0,3},{1,4},{2,5},{3,6},{4,7},{5,8},{6,9},{7,10},{8,11},{9,12},{10... | collective-permute-start | bytes 1572872 | tf_op jit(solution)/shard_map/ppermute | solution.py:20
  119.6 40.6 %collective-permute-start.17 = (bf16[512,512]{1,0:T(8,128)(2,1)}, bf16[512,512]{1,0:T(8,128)(2,1)}, u32[]{:S(2)}, u32[]{:S(2)}) collective-permute-start(bf16[512,512]{1,0:T(8,128)(2,1)} %get-tuple-element.53), channel_id=1, source_target_pairs={{7,0},{8,1},{9,2},{10,3},{11,4},{12,5},{13,6},{14,7},{15,8},{16,9}... | collective-permute-start | bytes 1572872 | tf_op jit(solution)/shard_map/ppermute | solution.py:20
  126.0 39.4 %collective-permute-start.18 = (bf16[512,512]{1,0:T(8,128)(2,1)}, bf16[512,512]{1,0:T(8,128)(2,1)}, u32[]{:S(2)}, u32[]{:S(2)}) collective-permute-start(bf16[512,512]{1,0:T(8,128)(2,1)} %get-tuple-element.54), channel_id=1, source_target_pairs={{0,7},{1,8},{2,9},{3,10},{4,11},{5,12},{6,13},{7,14},{8,15},{9,16}... | collective-permute-start | bytes 1572872 | tf_op jit(solution)/shard_map/ppermute | solution.py:20
  136.5 32.4 %collective-permute-start.19 = (bf16[512,512]{1,0:T(8,128)(2,1)}, bf16[512,512]{1,0:T(8,128)(2,1)}, u32[]{:S(2)}, u32[]{:S(2)}) collective-permute-start(bf16[512,512]{1,0:T(8,128)(2,1)} %get-tuple-element.55), channel_id=1, source_target_pairs={{5,0},{6,1},{7,2},{8,3},{9,4},{10,5},{11,6},{12,7},{13,8},{14,9},{... | collective-permute-start | bytes 1572872 | tf_op jit(solution)/shard_map/ppermute | solution.py:20
  139.2 32.0 %collective-permute-start.20 = (bf16[512,512]{1,0:T(8,128)(2,1)}, bf16[512,512]{1,0:T(8,128)(2,1)}, u32[]{:S(2)}, u32[]{:S(2)}) collective-permute-start(bf16[512,512]{1,0:T(8,128)(2,1)} %get-tuple-element.56), channel_id=1, source_target_pairs={{0,5},{1,6},{2,7},{3,8},{4,9},{5,10},{6,11},{7,12},{8,13},{9,14},{... | collective-permute-start | bytes 1572872 | tf_op jit(solution)/shard_map/ppermute | solution.py:20
  160.2 34.6 %collective-permute-start.22 = (bf16[512,512]{1,0:T(8,128)(2,1)}, bf16[512,512]{1,0:T(8,128)(2,1)}, u32[]{:S(2)}, u32[]{:S(2)}) collective-permute-start(bf16[512,512]{1,0:T(8,128)(2,1)} %copy-done.20), channel_id=1, source_target_pairs={{0,6},{1,7},{2,8},{3,9},{4,10},{5,11},{6,12},{7,13},{8,14},{9,15},... | collective-permute-start | bytes 1572872 | tf_op jit(solution)/shard_map/ppermute | solution.py:20
  165.4 29.4 %collective-permute-start.23 = (bf16[512,512]{1,0:T(8,128)(2,1)}, bf16[512,512]{1,0:T(8,128)(2,1)}, u32[]{:S(2)}, u32[]{:S(2)}) collective-permute-start(bf16[512,512]{1,0:T(8,128)(2,1)} %copy-done.19), channel_id=1, source_target_pairs={{2,0},{3,1},{4,2},{5,3},{6,4},{7,5},{8,6},{9,7},{10,8},{11,9},{12,... | collective-permute-start | bytes 1572872 | tf_op jit(solution)/shard_map/ppermute | solution.py:20
  168.9 25.9 %collective-permute-start.24 = (bf16[512,512]{1,0:T(8,128)(2,1)}, bf16[512,512]{1,0:T(8,128)(2,1)}, u32[]{:S(2)}, u32[]{:S(2)}) collective-permute-start(bf16[512,512]{1,0:T(8,128)(2,1)} %copy-done.18), channel_id=1, source_target_pairs={{0,2},{1,3},{2,4},{3,5},{4,6},{5,7},{6,8},{7,9},{8,10},{9,11},{10,... | collective-permute-start | bytes 1572872 | tf_op jit(solution)/shard_map/ppermute | solution.py:20
  201.4 28.2 %collective-permute-start.27 = (bf16[512,512]{1,0:T(8,128)(2,1)S(1)}, bf16[512,512]{1,0:T(8,128)(2,1)S(1)}, u32[]{:S(2)}, u32[]{:S(2)}) collective-permute-start(bf16[512,512]{1,0:T(8,128)(2,1)S(1)} %get-tuple-element.67), channel_id=1, source_target_pairs={{4,0},{5,1},{6,2},{7,3},{8,4},{9,5},{10,6},{11,7},{12,8},{13,9},{1... | collective-permute-start | bytes 1572872 | tf_op jit(solution)/shard_map/ppermute | solution.py:20
  209.5 28.3 %collective-permute-start.29 = (bf16[512,512]{1,0:T(8,128)(2,1)S(1)}, bf16[512,512]{1,0:T(8,128)(2,1)S(1)}, u32[]{:S(2)}, u32[]{:S(2)}) collective-permute-start(bf16[512,512]{1,0:T(8,128)(2,1)S(1)} %get-tuple-element.69), channel_id=1, source_target_pairs={{8,0},{9,1},{10,2},{11,3},{12,4},{13,5},{14,6},{15,7},{16,8},{17,9... | collective-permute-start | bytes 1572872 | tf_op jit(solution)/shard_map/ppermute | solution.py:20
  216.4 33.6 %collective-permute-start.30 = (bf16[512,512]{1,0:T(8,128)(2,1)S(1)}, bf16[512,512]{1,0:T(8,128)(2,1)S(1)}, u32[]{:S(2)}, u32[]{:S(2)}) collective-permute-start(bf16[512,512]{1,0:T(8,128)(2,1)S(1)} %get-tuple-element.70), channel_id=1, source_target_pairs={{0,8},{1,9},{2,10},{3,11},{4,12},{5,13},{6,14},{7,15},{8,16},{9,17... | collective-permute-start | bytes 1572872 | tf_op jit(solution)/shard_map/ppermute | solution.py:20
  218.4 36.8 %collective-permute-start.31 = (bf16[512,512]{1,0:T(8,128)(2,1)S(1)}, bf16[512,512]{1,0:T(8,128)(2,1)S(1)}, u32[]{:S(2)}, u32[]{:S(2)}) collective-permute-start(bf16[512,512]{1,0:T(8,128)(2,1)S(1)} %get-tuple-element.71), channel_id=1, source_target_pairs={{3,0},{4,1},{5,2},{6,3},{7,4},{8,5},{9,6},{10,7},{11,8},{12,9},{13... | collective-permute-start | bytes 1572872 | tf_op jit(solution)/shard_map/ppermute | solution.py:20
  229.6 36.8 %collective-permute-start.32 = (bf16[512,512]{1,0:T(8,128)(2,1)S(1)}, bf16[512,512]{1,0:T(8,128)(2,1)S(1)}, u32[]{:S(2)}, u32[]{:S(2)}) collective-permute-start(bf16[512,512]{1,0:T(8,128)(2,1)S(1)} %get-tuple-element.72), channel_id=1, source_target_pairs={{0,3},{1,4},{2,5},{3,6},{4,7},{5,8},{6,9},{7,10},{8,11},{9,12},{10... | collective-permute-start | bytes 1572872 | tf_op jit(solution)/shard_map/ppermute | solution.py:20
  231.7 36.6 %collective-permute-start.33 = (bf16[512,512]{1,0:T(8,128)(2,1)S(1)}, bf16[512,512]{1,0:T(8,128)(2,1)S(1)}, u32[]{:S(2)}, u32[]{:S(2)}) collective-permute-start(bf16[512,512]{1,0:T(8,128)(2,1)S(1)} %get-tuple-element.73), channel_id=1, source_target_pairs={{7,0},{8,1},{9,2},{10,3},{11,4},{12,5},{13,6},{14,7},{15,8},{16,9}... | collective-permute-start | bytes 1572872 | tf_op jit(solution)/shard_map/ppermute | solution.py:20
  237.9 43.4 %collective-permute-start.34 = (bf16[512,512]{1,0:T(8,128)(2,1)S(1)}, bf16[512,512]{1,0:T(8,128)(2,1)S(1)}, u32[]{:S(2)}, u32[]{:S(2)}) collective-permute-start(bf16[512,512]{1,0:T(8,128)(2,1)S(1)} %get-tuple-element.74), channel_id=1, source_target_pairs={{0,7},{1,8},{2,9},{3,10},{4,11},{5,12},{6,13},{7,14},{8,15},{9,16}... | collective-permute-start | bytes 1572872 | tf_op jit(solution)/shard_map/ppermute | solution.py:20
  250.1 33.1 %collective-permute-start.35 = (bf16[512,512]{1,0:T(8,128)(2,1)S(1)}, bf16[512,512]{1,0:T(8,128)(2,1)S(1)}, u32[]{:S(2)}, u32[]{:S(2)}) collective-permute-start(bf16[512,512]{1,0:T(8,128)(2,1)S(1)} %get-tuple-element.75), channel_id=1, source_target_pairs={{5,0},{6,1},{7,2},{8,3},{9,4},{10,5},{11,6},{12,7},{13,8},{14,9},{... | collective-permute-start | bytes 1572872 | tf_op jit(solution)/shard_map/ppermute | solution.py:20
  255.2 32.0 %collective-permute-start.36 = (bf16[512,512]{1,0:T(8,128)(2,1)S(1)}, bf16[512,512]{1,0:T(8,128)(2,1)S(1)}, u32[]{:S(2)}, u32[]{:S(2)}) collective-permute-start(bf16[512,512]{1,0:T(8,128)(2,1)S(1)} %get-tuple-element.76), channel_id=1, source_target_pairs={{0,5},{1,6},{2,7},{3,8},{4,9},{5,10},{6,11},{7,12},{8,13},{9,14},{... | collective-permute-start | bytes 1572872 | tf_op jit(solution)/shard_map/ppermute | solution.py:20
  266.3 35.2 %collective-permute-start.37 = (bf16[512,512]{1,0:T(8,128)(2,1)S(1)}, bf16[512,512]{1,0:T(8,128)(2,1)S(1)}, u32[]{:S(2)}, u32[]{:S(2)}) collective-permute-start(bf16[512,512]{1,0:T(8,128)(2,1)S(1)} %get-tuple-element.77), channel_id=1, source_target_pairs={{6,0},{7,1},{8,2},{9,3},{10,4},{11,5},{12,6},{13,7},{14,8},{15,9},... | collective-permute-start | bytes 1572872 | tf_op jit(solution)/shard_map/ppermute | solution.py:20
  268.3 43.1 %collective-permute-start.38 = (bf16[512,512]{1,0:T(8,128)(2,1)S(1)}, bf16[512,512]{1,0:T(8,128)(2,1)S(1)}, u32[]{:S(2)}, u32[]{:S(2)}) collective-permute-start(bf16[512,512]{1,0:T(8,128)(2,1)S(1)} %get-tuple-element.78), channel_id=1, source_target_pairs={{0,6},{1,7},{2,8},{3,9},{4,10},{5,11},{6,12},{7,13},{8,14},{9,15},... | collective-permute-start | bytes 1572872 | tf_op jit(solution)/shard_map/ppermute | solution.py:20
  281.3 30.1 %collective-permute-start.39 = (bf16[512,512]{1,0:T(8,128)(2,1)S(1)}, bf16[512,512]{1,0:T(8,128)(2,1)S(1)}, u32[]{:S(2)}, u32[]{:S(2)}) collective-permute-start(bf16[512,512]{1,0:T(8,128)(2,1)S(1)} %get-tuple-element.79), channel_id=1, source_target_pairs={{2,0},{3,1},{4,2},{5,3},{6,4},{7,5},{8,6},{9,7},{10,8},{11,9},{12,... | collective-permute-start | bytes 1572872 | tf_op jit(solution)/shard_map/ppermute | solution.py:20
  283.2 28.2 %collective-permute-start.40 = (bf16[512,512]{1,0:T(8,128)(2,1)S(1)}, bf16[512,512]{1,0:T(8,128)(2,1)S(1)}, u32[]{:S(2)}, u32[]{:S(2)}) collective-permute-start(bf16[512,512]{1,0:T(8,128)(2,1)S(1)} %get-tuple-element.80), channel_id=1, source_target_pairs={{0,2},{1,3},{2,4},{3,5},{4,6},{5,7},{6,8},{7,9},{8,10},{9,11},{10,... | collective-permute-start | bytes 1572872 | tf_op jit(solution)/shard_map/ppermute | solution.py:20
  (34 other events, 977.5 us)
